TPU v7x, 512 devices: a whole 4x8x8 slice. The times are simulated.
512 devices in a mesh: row: 16 (over x, z_lo), col: 32 (over y, z_hi, core).
Axes of the slice: x: 4, y: 8, z: 8 (z_hi: 2, z_lo: 4; z = z_hi * 4 + z_lo), core: 2. Of those that a mesh axis runs over, the one named last changes fastest.
Arguments:
- amplitudes: float32 [32, 96, 4, 128, 128], P('col', 'row'), may hold values from -6 to 6
- integrals: float32 [2, 2048, 16384], P(None, 'row', 'col'), may hold values from -0.25 to 0.25
- owner_column: int32 [2], replicated, may hold values from 0 to 31
- occ_irrep: int32 [96], replicated, may hold values from 0 to 7, as said below
- pair_irrep: int32 [2, 16], replicated, may hold values from 0 to 7, as said below
Outputs:
- ladder: float32 [12288, 16384], P('row', 'col')
Inputs may be any that keep to these rules, and one draw needn't show every extreme that they name: `occ_irrep`: every irrep 0 to 7 labels some occupied-pair tile. `pair_irrep`: in each section no irrep labels more than 4 of the 16 panel tiles, and some irrep labels exactly 4.
All inputs are finite; a program needn't handle non-finite values.
Results may differ from a plain program's by a relative error of at most 0.0001.
Values sent between devices are 32-bit elements; how exact they have to be, the bound alone decides.
A program may use at most 64 MiB of HBM per device.

v0:
```python
import jax
import jax.numpy as jnp
from jax import lax
from jax.sharding import PartitionSpec as P


def spread(value, axis, source):
    kept = jnp.where(lax.axis_index(axis) == source, value, 0).astype(value.dtype)
    return lax.psum(kept, axis)


def slot_tables(occ_labels, pair_labels, slot_count):
    matches = occ_labels[:, None] == pair_labels[None, :]
    order_rank = jnp.cumsum(matches.astype(jnp.int32), axis=1) - 1
    slot_ids = jnp.arange(slot_count, dtype=jnp.int32)
    chosen = matches[:, None, :] & (order_rank[:, None, :] == slot_ids[None, :, None])
    positions = jnp.arange(pair_labels.shape[0], dtype=jnp.int32)
    tile_index = jnp.sum(chosen.astype(jnp.int32) * positions[None, None, :], axis=2)
    valid_slot = jnp.any(chosen, axis=2)
    return (tile_index, valid_slot, chosen)


def on_device(amplitudes, integrals, owner_column, occ_irrep, pair_irrep):
    tiles_here = amplitudes.shape[1]
    slot_count = amplitudes.shape[2]
    tile_size = amplitudes.shape[3]
    section_count = integrals.shape[0]
    columns = integrals.shape[2]
    first_tile = lax.axis_index("row") * tiles_here
    occ_mine = lax.dynamic_slice_in_dim(occ_irrep, first_tile, tiles_here)

    def fetch_panel(which_section):
        return spread(amplitudes[0], "col", owner_column[which_section])

    tables = [
        slot_tables(occ_mine, pair_irrep[which_section], slot_count)
        for which_section in range(section_count)
    ]
    panels = [fetch_panel(which_section) for which_section in range(section_count)]
    section_rows = [
        lax.all_gather(integrals[which_section], "row", axis=0, tiled=True)
        for which_section in range(section_count)
    ]
    running = jnp.zeros((tiles_here, tile_size, columns), jnp.float32)
    for which_section in range(section_count):
        tile_index, valid_slot, chosen = tables[which_section]
        amp_panel = panels[which_section] * valid_slot[:, :, None, None].astype(jnp.float32)
        row_tiles = section_rows[which_section].reshape(-1, tile_size, columns)
        picked = jnp.take(row_tiles, tile_index, axis=0)
        running = running + jnp.einsum(
            "osij,osjv->oiv", amp_panel, picked, precision=lax.Precision.HIGHEST
        )
    return running.reshape(tiles_here * tile_size, columns)


def solution(mesh):
    return jax.shard_map(
        on_device,
        mesh=mesh,
        in_specs=(P("col", "row", None, None, None), P(None, "row", "col"), P(), P(), P()),
        out_specs=P("row", "col"),
        check_vma=False,
    )
```

profile of v0, /device:TPU:1, one launch (start us, length us, event | category | flops | bytes accessed | tf_op | source)
XLA Modules:
  0.0 477.0 jit_solution(14299060480379461248)
XLA Ops:
  7.4 0.0 copy-start.3
  7.4 0.0 copy-start.1
  7.4 0.0 all-gather.7.cloned.1.call-start
  7.4 2.0 fusion.24
  9.4 0.0 all-gather.7.cloned.1.call-update
  9.4 0.0 all-gather.5.cloned.1.call-start
  9.4 0.7 all-gather.5.cloned.1.call-update
  10.2 0.0 all-reduce.3.cloned.1.call-start
  10.2 0.0 copy-done.3
  10.2 0.6 fusion.25
  12.2 0.0 copy-done.1
  12.2 2.0 select_bitcast_fusion.1
  14.2 0.0 copy-start.5
  14.2 0.0 copy-start.4
  14.2 0.0 all-reduce.3.cloned.1.call-update
  14.3 0.6 copy-done.5
  14.9 0.1 dynamic_slice.3
  15.0 0.0 copy-done.4
  15.0 0.1 broadcast_compare_fusion.1
  15.1 0.2 reduce_window_sum.18
  15.2 0.2 select_reduce_fusion
  15.4 0.1 reshape.163
  15.5 0.2 fusion.18
  15.7 0.2 reduce_window_sum.17
  15.9 0.2 select_reduce_fusion.1
  16.1 0.1 reshape.159
  16.1 0.2 fusion.19
  16.4 133.2 %all-gather.7.cloned.1.call-done = f32[1,2048,512]{2,1,0:T(8,128)} async-done(((f32[1,128,512]{2,1,0:T(8,128)}), f32[1,2048,512]{2,1,0:T(8,128)}) %all-gather.7.cloned.1.call-update) | async-done | bytes 4194320 | tf_op jit(solution)/shard_map/all_gather | solution.py:41
  149.6 5.8 %gather_fusion.1 = f32[24,128,512]{2,1,0:T(8,128)} fusion(f32[16,128,512]{2,1,0:T(8,128)} %bitcast.23, s32[1024]{0:T(1024)S(1)} %pad_clamp_fusion), kind=kCustom, calls=%fused_computation.1.clone | custom fusion | bytes 12583008 | tf_op jit(solution)/shard_map/jit(_take)/gather | solution.py:49
  155.4 130.0 %all-gather.5.cloned.1.call-done = f32[1,2048,512]{2,1,0:T(8,128)} async-done(((f32[1,128,512]{2,1,0:T(8,128)}), f32[1,2048,512]{2,1,0:T(8,128)}) %all-gather.5.cloned.1.call-update) | async-done | bytes 4194320 | tf_op jit(solution)/shard_map/all_gather | solution.py:41
  285.4 5.8 %gather_fusion = f32[24,128,512]{2,1,0:T(8,128)} fusion(f32[16,128,512]{2,1,0:T(8,128)} %bitcast.24, s32[1024]{0:T(1024)S(1)} %pad_clamp_fusion.1), kind=kCustom, calls=%fused_computation.clone | custom fusion | bytes 12583008 | tf_op jit(solution)/shard_map/jit(_take)/gather | solution.py:49
  291.2 166.4 %all-reduce.3.cloned.1.call-done = (f32[6,4,128,128]{3,2,1,0:T(8,128)}, f32[6,4,128,128]{3,2,1,0:T(8,128)}) async-done(((f32[6,4,128,128]{3,2,1,0:T(8,128)}, f32[6,4,128,128]{3,2,1,0:T(8,128)}), (f32[6,4,128,128]{3,2,1,0:T(8,128)}, f32[6,4,128,128]{3,2,1,0:T(8,128)})) %all-reduce.3.cloned.1.call-update) | async-done | bytes 3145744 | tf_op jit(solution)/shard_map/psum | solution.py:9
  457.6 0.0 copy-start
  457.6 0.0 copy-start.2
  457.6 6.9 %fusion = f32[6,128,512,1]{2,1,3,0:T(8,128)S(1)} fusion(f32[6,4,128,512]{3,2,1,0:T(8,128)} %bitcast.21, pred[6,4]{1,0:T(8,128)(4,1)S(1)} %compare_and_fusion, f32[6,4,128,128]{3,2,1,0:T(8,128)} %get-tuple-element.6, f32[6,4]{1,0:T(8,128)S(1)} %convert_element_type.38), kind=kOutput, calls=%fused_computation.2 | convolution fusion | flops 2417885184 | bytes 9437304 | tf_op jit(solution)/shard_map/osij,osjv->oiv/dot_general | solution.py:50
  464.6 0.0 copy-done
  464.6 0.0 copy-done.2
  464.6 5.0 %bitcast_add_fusion = f32[6,128,512]{2,1,0:T(8,128)} fusion(f32[6,128,512,1]{2,1,3,0:T(8,128)S(1)} %fusion, f32[6,4,128,512]{3,2,1,0:T(8,128)S(1)} %bitcast.22, pred[6,4]{1,0:T(8,128)(4,1)S(1)} %compare_and_fusion.1, f32[6,4,128,128]{3,2,1,0:T(8,128)S(1)} %copy-done.2, f32[6,4]{1,0:T(8,128)S(1)} %convert_element_type.36), kind=kOutput, calls=%fused_computation.10 | convolution fusion | flops 2418278400 | bytes 11010168 | tf_op jit(solution)/shard_map/osij,osjv->oiv/dot_general | solution.py:50
  (11 shorter events, 0.1 us)
Async XLA Ops:
  7.4 2.8 copy-start.3
  7.4 4.8 %copy-start.1 = (f32[1,6,4,128,128]{4,3,2,1,0:T(8,128)S(1)}, f32[1,6,4,128,128]{4,3,2,1,0:T(8,128)}, u32[]{:S(2)}) copy-start(f32[1,6,4,128,128]{4,3,2,1,0:T(8,128)} %param.7) | copy-start | bytes 4718596
  7.4 142.2 %all-gather.7.cloned.1.call-start = ((), (), s32[]{:S(2)}) async-start(), calls=%async_computation.1 | async-start | bytes 4456448 | tf_op jit(solution)/shard_map/all_gather | solution.py:41
  9.4 276.0 %all-gather.5.cloned.1.call-start = ((), (), s32[]{:S(2)}) async-start(), calls=%async_computation | async-start | bytes 4456448 | tf_op jit(solution)/shard_map/all_gather | solution.py:41
  10.2 447.5 %all-reduce.3.cloned.1.call-start = ((), (), s32[]{:S(2)}) async-start(), calls=%async_computation.2 | async-start | bytes 6291456 | tf_op jit(solution)/shard_map/psum | solution.py:9
  14.2 0.7 copy-start.5
  14.2 0.7 copy-start.4
  457.6 7.0 %copy-start = (f32[24,128,512]{2,1,0:T(8,128)S(1)}, f32[24,128,512]{2,1,0:T(8,128)}, u32[]{:S(2)}) copy-start(f32[24,128,512]{2,1,0:T(8,128)} %gather_fusion) | copy-start | bytes 18874372
  457.6 7.0 %copy-start.2 = (f32[6,4,128,128]{3,2,1,0:T(8,128)S(1)}, f32[6,4,128,128]{3,2,1,0:T(8,128)}, u32[]{:S(2)}) copy-start(f32[6,4,128,128]{3,2,1,0:T(8,128)} %get-tuple-element.7) | copy-start | bytes 4718596
Sparse Core Ops, SparseCore 0:
  10.3 139.2 all-gather.6
  151.9 133.4 all-gather.4
Sparse Core Ops, SparseCore 1:
  14.4 443.2 all-reduce.2
where the time goes:
time: 477 us
  waiting for transfers between devices  430 us (90%)
  between operations  16.3 us (3%)
  local copies, waits for them, and re-layouts  15.1 us (3%)
  matrix products  12 us (3%)
    all_gather x2, waiting for transfers between devices, on_device(): lax.all_gather(integrals[which_section], 'row', axis=0, tiled=True)  263 us
    psum x1, waiting for transfers between devices, spread(): return lax.psum(kept, axis)  166 us
    dot_general x2, matrix products, on_device(): jnp.einsum('osij,osjv->oiv', amp_panel, picked, precision=lax.Precision.H...  12 us
    gather x2, local copies, waits for them, and re-layouts, on_device(): picked = jnp.take(row_tiles, tile_index, axis=0)  11.6 us
  transfers between devices with their start and end apart: 3, of which 3 were waited for; matrix products, arithmetic and copies ran while one was open for 3% of the time, Pallas kernels for 0%

commit v1 on v0

--- a/solution.py
+++ b/solution.py
@@ -2,6 +2,17 @@
 import jax.numpy as jnp
 from jax import lax
 from jax.sharding import PartitionSpec as P
+
+
+def _name_works(array_in):
+    mat_out = lax.all_to_all(
+        jnp.stack([array_in] * lax.axis_size("row"), axis=0),
+        split_axis=0,
+        axis_name="row",
+        concat_axis=0,
+    )
+    far_arr = jnp.concatenate(mat_out, axis=0)
+    return far_arr
 
 
 def spread(value, axis, source):
@@ -37,10 +48,7 @@
         for which_section in range(section_count)
     ]
     panels = [fetch_panel(which_section) for which_section in range(section_count)]
-    section_rows = [
-        lax.all_gather(integrals[which_section], "row", axis=0, tiled=True)
-        for which_section in range(section_count)
-    ]
+    section_rows = [_name_works(integrals[which_section]) for which_section in range(section_count)]
     running = jnp.zeros((tiles_here, tile_size, columns), jnp.float32)
     for which_section in range(section_count):
         tile_index, valid_slot, chosen = tables[which_section]

time: 477 us -> 552 us (1.16)
  blocking collectives: 0 us -> 105 us
  waiting for transfers between devices: 430 us -> 393 us
    all_gather x2 -> x0, waiting for transfers between devices: 263 us -> none  [on_device(): lax.all_gather(integrals[which_section], 'row', axis=0, tiled=True)]
    psum x1, waiting for transfers between devices: 166 us -> 393 us  [spread(): return lax.psum(kept, axis)]
    all_to_all x0 -> x1, blocking collectives: none -> 105 us  [_name_works(): lax.all_to_all(jnp.stack([array_in] * lax.axis_size('row'), axis=0), spli...]
  transfers between devices with their start and end apart: 3 -> 2, of which waited for: 3 -> 1; matrix products, arithmetic and copies ran while one was open for 3% -> 3% of each run, Pallas kernels for 0% -> 0%
where the time goes in v1:
time: 552 us; the launch traced here: 551 us
  waiting for transfers between devices  393 us (71%)
  blocking collectives  105 us (19%)
  local copies, waits for them, and re-layouts  17.4 us (3%)
  between operations  14.9 us (3%)
  matrix products  13.7 us (2%)
    psum x1, waiting for transfers between devices, spread(): return lax.psum(kept, axis)  393 us
    all_to_all x1, blocking collectives, _name_works(): lax.all_to_all(jnp.stack([array_in] * lax.axis_size('row'), axis=0), spli...  105 us
    dot_general x2, matrix products, on_device(): jnp.einsum('osij,osjv->oiv', amp_panel, picked, precision=lax.Precision.H...  13.7 us
    gather x2, local copies, waits for them, and re-layouts, on_device(): picked = jnp.take(row_tiles, tile_index, axis=0)  11.7 us
  transfers between devices with their start and end apart: 2, of which 1 were waited for; matrix products, arithmetic and copies ran while one was open for 3% of the time, Pallas kernels for 0%

profile of v1, /device:TPU:1, one launch (start us, length us, event | category | flops | bytes accessed | tf_op | source)
XLA Modules:
  0.0 551.4 jit_solution(6765733735056756164)
XLA Ops:
  6.5 1.1 slice_bitcast_fusion.1
  7.6 0.5 stack.7
  8.1 104.6 %all_to_all.10 = f32[16,128,512]{2,1,0:T(8,128)} all-to-all(f32[16,128,512]{2,1,0:T(8,128)S(1)} %stack.7), channel_id=1, replica_groups=mesh['row'=16,'col'=32] {'row'}, dimensions={0} | all-to-all | bytes 8388608 | tf_op jit(solution)/shard_map/all_to_all | solution.py:8
  112.8 2.6 stack.6
  115.4 0.0 copy-start.2
  115.4 0.0 copy-start
  115.4 4.7 all-to-all-start
  120.1 0.0 all-reduce.3.cloned.1.call-start
  120.1 0.0 copy-done.2
  120.1 0.7 fusion.24
  122.2 0.0 copy-done
  122.2 2.1 select_bitcast_fusion.1
  124.3 0.0 copy-start.4
  124.3 0.0 copy-start.3
  124.3 0.0 all-reduce.3.cloned.1.call-update
  124.3 0.6 copy-done.4
  124.9 0.1 dynamic_slice.3
  125.0 0.0 copy-done.3
  125.0 0.1 broadcast_compare_fusion.1
  125.1 0.2 reduce_window_sum.18
  125.2 0.2 select_reduce_fusion
  125.4 0.1 reshape.153
  125.5 0.2 fusion.18
  125.7 0.2 reduce_window_sum.17
  125.9 0.2 select_reduce_fusion.1
  126.1 0.1 reshape.149
  126.2 0.2 fusion.19
  126.4 5.8 %gather_fusion.1 = f32[24,128,512]{2,1,0:T(8,128)} fusion(f32[16,128,512]{2,1,0:T(8,128)} %all_to_all.10, s32[1024]{0:T(1024)S(1)} %pad_clamp_fusion), kind=kCustom, calls=%fused_computation.1.clone | custom fusion | bytes 12583008 | tf_op jit(solution)/shard_map/jit(_take)/gather | solution.py:57
  132.2 392.7 %all-reduce.3.cloned.1.call-done = (f32[6,4,128,128]{3,2,1,0:T(8,128)}, f32[6,4,128,128]{3,2,1,0:T(8,128)}) async-done(((f32[6,4,128,128]{3,2,1,0:T(8,128)}, f32[6,4,128,128]{3,2,1,0:T(8,128)}), (f32[6,4,128,128]{3,2,1,0:T(8,128)}, f32[6,4,128,128]{3,2,1,0:T(8,128)})) %all-reduce.3.cloned.1.call-update) | async-done | bytes 3145744 | tf_op jit(solution)/shard_map/psum | solution.py:20
  525.0 6.8 %fusion = f32[6,128,512,1]{2,1,3,0:T(8,128)S(1)} fusion(f32[6,4,128,512]{3,2,1,0:T(8,128)} %bitcast.23, pred[6,4]{1,0:T(8,128)(4,1)S(1)} %compare_and_fusion, f32[6,4,128,128]{3,2,1,0:T(8,128)} %get-tuple-element.6, f32[6,4]{1,0:T(8,128)S(1)} %convert_element_type.38), kind=kOutput, calls=%fused_computation.2 | convolution fusion | flops 2417885184 | bytes 9437304 | tf_op jit(solution)/shard_map/osij,osjv->oiv/dot_general | solution.py:58
  531.8 0.0 copy-start.1
  531.8 0.0 all-to-all-done
  531.8 5.9 %gather_fusion = f32[24,128,512]{2,1,0:T(8,128)} fusion(f32[16,128,512]{2,1,0:T(8,128)} %all-to-all-done, s32[1024]{0:T(1024)S(1)} %pad_clamp_fusion.1), kind=kCustom, calls=%fused_computation.clone | custom fusion | bytes 12583008 | tf_op jit(solution)/shard_map/jit(_take)/gather | solution.py:57
  537.7 0.0 copy-done.1
  537.7 6.9 %bitcast_add_fusion = f32[6,128,512]{2,1,0:T(8,128)} fusion(f32[6,128,512,1]{2,1,3,0:T(8,128)S(1)} %fusion, f32[6,4,128,512]{3,2,1,0:T(8,128)} %bitcast.24, pred[6,4]{1,0:T(8,128)(4,1)S(1)} %compare_and_fusion.1, f32[6,4,128,128]{3,2,1,0:T(8,128)S(1)} %copy-done.1, f32[6,4]{1,0:T(8,128)S(1)} %convert_element_type.36), kind=kOutput, calls=%fused_computation.10 | convolution fusion | flops 2418278400 | bytes 11010168 | tf_op jit(solution)/shard_map/osij,osjv->oiv/dot_general | solution.py:58
  (11 shorter events, 0.1 us)
Async XLA Ops:
  115.4 4.7 copy-start.2
  115.4 6.8 %copy-start = (f32[1,6,4,128,128]{4,3,2,1,0:T(8,128)S(1)}, f32[1,6,4,128,128]{4,3,2,1,0:T(8,128)}, u32[]{:S(2)}) copy-start(f32[1,6,4,128,128]{4,3,2,1,0:T(8,128)} %param.7) | copy-start | bytes 4718596
  115.4 416.4 %all-to-all-start = ((f32[16,128,512]{2,1,0:T(8,128)}), f32[16,128,512]{2,1,0:T(8,128)}, u32[]{:S(2)}, u32[]{:S(2)}) async-start(f32[16,128,512]{2,1,0:T(8,128)} %stack.6), calls=%async_computation | async-start | bytes 8388608 | tf_op jit(solution)/shard_map/all_to_all | solution.py:8
  120.1 404.9 %all-reduce.3.cloned.1.call-start = ((), (), s32[]{:S(2)}) async-start(), calls=%async_computation.2 | async-start | bytes 6291456 | tf_op jit(solution)/shard_map/psum | solution.py:20
  124.3 0.7 copy-start.4
  124.3 0.7 copy-start.3
  531.8 5.9 %copy-start.1 = (f32[6,4,128,128]{3,2,1,0:T(8,128)S(1)}, f32[6,4,128,128]{3,2,1,0:T(8,128)}, u32[]{:S(2)}) copy-start(f32[6,4,128,128]{3,2,1,0:T(8,128)} %get-tuple-element.7) | copy-start | bytes 4718596
Sparse Core Ops, SparseCore 0:
  124.4 400.5 all-reduce.2
